TPU v7x, 32 devices: a whole 2x2x4 slice. The times are simulated.
32 devices in a mesh: group: 2 (over y), seq: 4 (over z), req: 2 (over x), sub: 2 (over core).
Axes of the slice: x: 2, y: 2, z: 4, core: 2. Of those that a mesh axis runs over, the one named last changes fastest.
Arguments:
- latent_codes: bfloat16 [2, 16, 2048, 512], P(None, ('group', 'req', 'sub'), 'seq'), parts along dimension 1, may hold values from -6 to 6
- latent_scales: bfloat16 [2, 16, 2048, 4], P(None, ('group', 'req', 'sub'), 'seq'), parts along dimension 1, may hold values from 0.34 to 3.5
- rope_keys: bfloat16 [2, 16, 2048, 64], P(None, ('group', 'req', 'sub'), 'seq'), parts along dimension 1, may hold values from -6 to 6
- lengths: int32 [16], P(('group', 'req', 'sub')), parts along dimension 0, may hold values from 256 to 2048, as said below
- query_latent: bfloat16 [2, 16, 4, 128, 512], P(None, ('group', 'req', 'sub'), None, 'seq'), parts along dimension 1, may hold values from -64 to 64
- query_rope: bfloat16 [2, 16, 4, 128, 64], P(None, ('group', 'req', 'sub'), None, 'seq'), parts along dimension 1, may hold values from -8 to 8
- new_latent: bfloat16 [2, 16, 4, 512], P(None, ('group', 'req', 'sub')), parts along dimension 1, may hold values from -9 to 9
- new_rope: bfloat16 [2, 16, 4, 64], P(None, ('group', 'req', 'sub')), parts along dimension 1, may hold values from -6 to 6
Outputs:
- attended: bfloat16 [2, 16, 4, 128, 512], P(None, ('group', 'req', 'sub'), None, 'seq'), parts along dimension 1
- cache_codes: bfloat16 [2, 16, 512, 4, 512], P(None, ('group', 'req', 'sub'), None, 'seq'), parts along dimension 1
- cache_scales: bfloat16 [2, 16, 512, 4, 4], P(None, ('group', 'req', 'sub'), None, 'seq'), parts along dimension 1
- cache_rope: bfloat16 [2, 16, 512, 4, 64], P(None, ('group', 'req', 'sub'), None, 'seq'), parts along dimension 1
There are 2 independent parts, one for each index of `group`. A program takes and returns all parts, laid end to end along the dimension named above; each array names one. Nothing has to cross between parts.
Inputs may be any that keep to these rules, and one draw needn't show every extreme that they name: `lengths`: one request is exactly 2048 long.
All inputs are finite; a program needn't handle non-finite values.
Results may differ from a plain program's by a relative error of at most 0.013.
Values may be sent and summed in bfloat16 or wider, within the bound.
A program may use at most 64 MiB of HBM per device.

v0:
```python
import jax
import jax.numpy as jnp
from jax import lax
from jax.sharding import PartitionSpec as P

softmax_gain = 192.0 ** (-0.5)
masked_score = -1e30


def dequantize(code_values, scale_values):
    blocks = scale_values.shape[-1]
    latent_width = code_values.shape[-1]
    shaped = code_values.astype(jnp.float32).reshape(
        code_values.shape[:-1] + (blocks, latent_width // blocks)
    )
    scaled = shaped * scale_values.astype(jnp.float32)[..., None]
    return scaled.reshape(code_values.shape).astype(jnp.bfloat16)


def shard_partial(
    lat_query, rope_query, key_rows, rope_rows, usable, new_keys, new_rope_rows, holds_new
):
    tokens_new, head_count, latent_width = lat_query.shape
    query_rows = lat_query.reshape(tokens_new * head_count, latent_width)
    query_pos = rope_query.reshape(tokens_new * head_count, rope_query.shape[-1])
    scores = jnp.dot(query_rows, key_rows.T, preferred_element_type=jnp.float32)
    scores = (
        scores + jnp.dot(query_pos, rope_rows.T, preferred_element_type=jnp.float32)
    ) * softmax_gain
    fresh_scores = jnp.dot(query_rows, new_keys.T, preferred_element_type=jnp.float32)
    fresh_scores = (
        fresh_scores + jnp.dot(query_pos, new_rope_rows.T, preferred_element_type=jnp.float32)
    ) * softmax_gain
    token_of_row = jnp.arange(tokens_new * head_count, dtype=jnp.int32) // head_count
    causal = (jnp.arange(tokens_new, dtype=jnp.int32)[None, :] <= token_of_row[:, None]) & holds_new
    scores = jnp.where(usable[None, :], scores, masked_score)
    fresh_scores = jnp.where(causal, fresh_scores, masked_score)
    group_peak = jnp.maximum(jnp.max(scores, 1), jnp.max(fresh_scores, 1)).astype(jnp.bfloat16)
    peak_float = group_peak.astype(jnp.float32)[:, None]
    weights = jnp.where(usable[None, :], jnp.exp(scores - peak_float), 0.0).astype(jnp.bfloat16)
    fresh_weights = jnp.where(causal, jnp.exp(fresh_scores - peak_float), 0.0).astype(jnp.bfloat16)
    group_total = jnp.sum(weights.astype(jnp.float32), 1) + jnp.sum(
        fresh_weights.astype(jnp.float32), 1
    )
    group_sum = jnp.dot(weights, key_rows, preferred_element_type=jnp.float32)
    group_sum = group_sum + jnp.dot(fresh_weights, new_keys, preferred_element_type=jnp.float32)
    return (
        group_sum.astype(jnp.bfloat16).reshape(tokens_new, head_count, latent_width),
        group_peak.reshape(tokens_new, head_count),
        group_total.astype(jnp.bfloat16).reshape(tokens_new, head_count),
    )


def merge_groups(pieces):
    group_sum, group_peak, group_total = pieces
    peak_float = group_peak.astype(jnp.float32)
    overall = jnp.max(peak_float, 0)
    factor = jnp.exp(peak_float - overall)
    numerator = jnp.sum(factor[..., None] * group_sum.astype(jnp.float32), 0)
    denominator = jnp.sum(factor * group_total.astype(jnp.float32), 0)
    return (numerator / denominator[..., None]).astype(jnp.bfloat16)


def per_device(
    latent_codes, latent_scales, rope_keys, lengths, query_latent, query_rope, new_latent, new_rope
):
    shard_count = lax.axis_size("seq")
    seq_index = lax.axis_index("seq")
    layer_count, request_count, span, latent_width = latent_codes.shape
    lat_query, rope_query = (
        lax.all_gather(query_latent, "seq", axis=3, tiled=True),
        lax.all_gather(query_rope, "seq", axis=3, tiled=True),
    )

    def regroup_rows(values):
        return values.reshape(
            values.shape[0], values.shape[1], span // shard_count, shard_count, values.shape[-1]
        )

    codes_moved, scales_moved, rope_moved = (
        lax.all_to_all(regroup_rows(latent_codes), "seq", split_axis=3, concat_axis=2, tiled=True),
        lax.all_to_all(regroup_rows(latent_scales), "seq", split_axis=3, concat_axis=2, tiled=True),
        lax.all_to_all(regroup_rows(rope_keys), "seq", split_axis=3, concat_axis=2, tiled=True),
    )
    offsets = jnp.arange(span, dtype=jnp.int32)
    key_rows = dequantize(latent_codes, latent_scales)
    positions = seq_index * span + offsets
    usable = positions[None, :] < lengths[:, None]
    holds_new = seq_index == 0
    per_request = jax.vmap(shard_partial, in_axes=(0, 0, 0, 0, 0, 0, 0, None))
    per_layer = jax.vmap(per_request, in_axes=(0, 0, 0, 0, None, 0, 0, None))
    group_sum, group_peak, group_total = per_layer(
        lat_query, rope_query, key_rows, rope_keys, usable, new_latent, new_rope, holds_new
    )
    attended = merge_groups(
        (
            lax.all_to_all(group_sum[None], "seq", split_axis=4, concat_axis=0, tiled=True),
            lax.all_to_all(group_peak[None], "seq", split_axis=4, concat_axis=0, tiled=True),
            lax.all_to_all(group_total[None], "seq", split_axis=4, concat_axis=0, tiled=True),
        )
    )
    return (attended, codes_moved, scales_moved, rope_moved)


def solution(mesh):
    placed = (
        P(None, ("group", "req", "sub"), "seq", None),
        P(None, ("group", "req", "sub"), "seq", None),
        P(None, ("group", "req", "sub"), "seq", None),
        P(("group", "req", "sub")),
        P(None, ("group", "req", "sub"), None, "seq", None),
        P(None, ("group", "req", "sub"), None, "seq", None),
        P(None, ("group", "req", "sub"), None, None),
        P(None, ("group", "req", "sub"), None, None),
    )
    return jax.shard_map(
        per_device,
        mesh=mesh,
        in_specs=placed,
        out_specs=(
            P(None, ("group", "req", "sub"), None, "seq", None),
            P(None, ("group", "req", "sub"), None, "seq", None),
            P(None, ("group", "req", "sub"), None, "seq", None),
            P(None, ("group", "req", "sub"), None, "seq", None),
        ),
        check_vma=False,
    )
```

profile of v0, /device:TPU:0, one launch (start us, length us, event | category | flops | bytes accessed | tf_op | source)
XLA Modules:
  0.0 215.6 jit_solution(11127280630018597931)
XLA Ops:
  7.2 0.0 copy-start
  7.2 0.0 all-gather.2.cloned.1.call-start
  7.2 0.7 all-gather.2.cloned.1.call-update
  7.9 1.8 reshape.126
  9.8 0.8 copy.66
  10.6 6.3 %all-to-all-start.4 = ((bf16[2,2,128,4,4]{2,4,1,0,3:T(4,128)(2,1)}), bf16[2,2,128,4,4]{2,4,1,0,3:T(4,128)(2,1)S(1)}, u32[]{:S(2)}, u32[]{:S(2)}) async-start(bf16[2,2,128,4,4]{2,4,1,0,3:T(4,128)(2,1)} %copy.66), calls=%async_computation.4 | async-start | bytes 32768 | tf_op jit(solution)/shard_map/all_to_all | solution.py:82
  16.9 1.2 copy.68
  18.1 1.0 copy.69
  19.2 3.4 %all-to-all-done.4 = bf16[2,2,128,4,4]{2,4,1,0,3:T(4,128)(2,1)S(1)} async-done(((bf16[2,2,128,4,4]{2,4,1,0,3:T(4,128)(2,1)}), bf16[2,2,128,4,4]{2,4,1,0,3:T(4,128)(2,1)S(1)}, u32[]{:S(2)}, u32[]{:S(2)}) %all-to-all-start.4) | async-done | bytes 16416 | tf_op jit(solution)/shard_map/all_to_all | solution.py:82
  22.5 3.4 %all-to-all-start.5 = ((bf16[2,2,128,4,64]{2,4,1,0,3:T(8,128)(2,1)}), bf16[2,2,128,4,64]{2,4,1,0,3:T(8,128)(2,1)S(1)}, u32[]{:S(2)}, u32[]{:S(2)}) async-start(bf16[2,2,128,4,64]{2,4,1,0,3:T(8,128)(2,1)} %copy.69), calls=%async_computation.5 | async-start | bytes 524288 | tf_op jit(solution)/shard_map/all_to_all | solution.py:83
  25.9 1.0 copy.57
  26.9 3.9 %mul.38 = f32[2,2,512,4,128]{4,3,2,1,0:T(4,128)} broadcast(f32[2,2,512,4]{3,2,1,0:T(8,128)S(1)} %copy.57), dimensions={0,1,2,3} | broadcast | bytes 4227072 | tf_op jit(solution)/shard_map/mul | solution.py:16
  30.8 5.6 %mul.39 = f32[2,2,512,512]{3,2,1,0:T(8,128)} reshape(f32[2,2,512,4,128]{4,3,2,1,0:T(4,128)} %mul.38) | data formatting | bytes 8388608 | tf_op jit(solution)/shard_map/mul | solution.py:16
  36.4 2.2 %copy.63 = bf16[2,2,512,512]{3,1,2,0:T(2,128)(2,1)S(1)} copy(bf16[2,2,512,512]{3,2,1,0:T(8,128)(2,1)S(1)} %copy-done.2) | data formatting | bytes 4194304 | tf_op args[0]
  38.6 0.0 copy-start.4
  38.6 0.0 copy-start.6
  38.6 2.0 copy.64
  40.6 1.7 all-to-all-done.5
  42.3 4.5 %all-to-all-start.3 = ((bf16[2,2,128,4,512]{4,2,1,0,3:T(8,128)(2,1)}), bf16[2,2,128,4,512]{4,2,1,0,3:T(8,128)(2,1)}, u32[]{:S(2)}, u32[]{:S(2)}) async-start(bf16[2,2,128,4,512]{4,2,1,0,3:T(8,128)(2,1)} %copy.64), calls=%async_computation.3 | async-start | bytes 4194304 | tf_op jit(solution)/shard_map/all_to_all | solution.py:81
  46.8 71.2 %all_gather.7 = bf16[2,2,4,128,64]{4,3,2,1,0:T(8,128)(2,1)S(1)} all-gather(bf16[2,2,4,32,64]{4,3,2,1,0:T(8,128)(2,1)S(1)} %copy-done.4), channel_id=1, replica_groups=mesh['group'=2,'seq'=4,'req'=2,'sub'=2] {'seq'}, dimensions={3}, use_global_device_ids=true | all-gather | bytes 327680 | tf_op jit(solution)/shard_map/all_gather | solution.py:72
  118.0 0.1 broadcast_compare_fusion
  118.1 0.2 fusion.17
  118.3 2.8 %fusion.16 = f32[2,2,512,512]{2,3,1,0:T(8,128)} fusion(bf16[2,2,512,64]{3,2,1,0:T(8,128)(2,1)S(1)} %bitcast.77, bf16[2,2,512,64]{2,3,1,0:T(8,128)(2,1)S(1)} %copy-done.3), kind=kOutput, calls=%fused_computation.39 | convolution fusion | flops 134217728 | bytes 4718592 | tf_op jit(solution)/shard_map/vmap(vmap())/dot_general | solution.py:28
  121.1 2.3 %fusion.15 = (bf16[2,2,512]{2,1,0:T(2,128)(2,1)S(1)}, f32[2,2,512,4]{2,3,1,0:T(4,128)S(1)}) fusion(f32[2,2,512,4]{2,3,1,0:T(4,128)S(1)} %fusion.17, bf16[2,2,512,512]{3,2,1,0:T(8,128)(2,1)} %bitcast.74, bf16[2,2,4,512]{3,2,1,0:T(4,128)(2,1)S(1)} %copy-done, pred[512,4]{0,1:T(4,128)(4,1)S(1)} %fusion.8), kind=kOutput, calls=%fused_computation.38 | convolution fusion | flops 8419328 | bytes 2185216 | tf_op jit(solution)/shard_map/vmap(vmap())/dot_general | solution.py:30
  123.4 5.6 %fusion.14 = (bf16[2,2,512]{2,1,0:T(2,128)(2,1)S(1)}, f32[2,2,512,512]{2,3,1,0:T(8,128)S(1)}) fusion(f32[2,2,512,512]{2,3,1,0:T(8,128)} %fusion.16, bf16[2,2,512,512]{3,2,1,0:T(8,128)(2,1)} %bitcast.75, f32[2,2,512,512]{3,2,1,0:T(8,128)} %mul.39, bf16[2,2,512,512]{3,2,1,0:T(8,128)(2,1)S(1)} %copy-done.2, pred[2,512]{1,0:T(4,128)(4,1)S(1)} %broadcast_compare_fusion), kind=kOutput, calls=%fused_computation.37 | convolution fusion | flops 1081079808 | bytes 16782336 | tf_op jit(solution)/shard_map/vmap(vmap())/dot_general | solution.py:26
  129.0 1.9 copy-done.1
  130.9 0.7 convert_reduce_fusion
  131.7 0.2 copy.62
  131.9 0.8 reshape.135
  132.7 5.0 %all-to-all-start.2 = ((bf16[4,2,256]{2,1,0:T(2,128)(2,1)}), bf16[4,2,256]{2,1,0:T(2,128)(2,1)S(1)}, u32[]{:S(2)}, u32[]{:S(2)}) async-start(bf16[4,2,256]{2,1,0:T(2,128)(2,1)} %reshape.135), calls=%async_computation.2 | async-start | bytes 8192 | tf_op jit(solution)/shard_map/all_to_all | solution.py:99
  137.6 7.1 %fusion.5 = f32[2,2,512,512]{3,2,1,0:T(8,128)} fusion(f32[2,2,512,512]{2,3,1,0:T(8,128)} %copy-done.1, f32[2,2,512]{2,1,0:T(2,128)S(1)} %get-tuple-element.20, pred[2,512]{1,0:T(4,128)(4,1)S(1)} %broadcast_compare_fusion, f32[2,2,512,512]{3,2,1,0:T(8,128)} %mul.39, bf16[2,2,512,512]{3,2,1,0:T(8,128)(2,1)S(1)} %copy-done.2), kind=kOutput, calls=%fused_computation.13 | convolution fusion | flops 1080033280 | bytes 14689280 | tf_op jit(solution)/shard_map/vmap(vmap())/dot_general | solution.py:45
  144.8 0.2 copy.59
  145.0 0.8 reshape.133
  145.7 5.1 %all-to-all-start = ((bf16[4,2,256]{2,1,0:T(2,128)(2,1)}), bf16[4,2,256]{2,1,0:T(2,128)(2,1)S(1)}, u32[]{:S(2)}, u32[]{:S(2)}) async-start(bf16[4,2,256]{2,1,0:T(2,128)(2,1)} %reshape.133), calls=%async_computation | async-start | bytes 8192 | tf_op jit(solution)/shard_map/all_to_all | solution.py:98
  150.8 3.0 %add_convert_fusion = bf16[2,2,512,512]{3,2,1,0:T(8,128)(2,1)S(1)} fusion(f32[2,2,512,512]{3,2,1,0:T(8,128)} %fusion.5, bf16[2,2,4,512]{3,2,1,0:T(4,128)(2,1)S(1)} %copy-done, f32[2,2,512,4]{2,3,1,0:T(4,128)S(1)} %get-tuple-element.27, f32[2,2,512]{2,1,0:T(2,128)S(1)} %get-tuple-element.20, pred[512,4]{0,1:T(4,128)(4,1)S(1)} %fusion.8), kind=kOutput, calls=%fused_computation.6 | convolution fusion | flops 10510336 | bytes 6350848 | tf_op jit(solution)/shard_map/vmap(vmap())/dot_general | solution.py:46
  153.8 3.0 %copy.61 = bf16[1,2,2,4,128,512]{5,3,2,1,0,4:T(4,128)(2,1)} copy(bf16[1,2,2,4,128,512]{5,4,3,2,1,0:T(8,128)(2,1)S(1)} %bitcast.72) | data formatting | bytes 4194304 | tf_op jit(solution)/shard_map/broadcast_in_dim;vmap(vmap())/reshape | solution.py:97
  156.8 5.1 %all-to-all-start.1 = ((bf16[1,2,2,4,128,512]{5,3,2,1,0,4:T(4,128)(2,1)}), bf16[1,2,2,4,128,512]{5,3,2,1,0,4:T(4,128)(2,1)S(1)}, u32[]{:S(2)}, u32[]{:S(2)}) async-start(bf16[1,2,2,4,128,512]{5,3,2,1,0,4:T(4,128)(2,1)} %copy.61), calls=%async_computation.1 | async-start | bytes 4194304 | tf_op jit(solution)/shard_map/all_to_all | solution.py:97
  161.9 0.6 copy_bitcast_fusion
  162.5 0.7 bitcast_bitcast_fusion
  163.2 3.1 %copy.65 = bf16[2,2,128,4,512]{4,2,3,1,0:T(8,128)(2,1)} copy(bf16[2,2,128,4,512]{4,2,1,0,3:T(8,128)(2,1)} %all-to-all-done.3) | data formatting | bytes 4194304 | tf_op jit(solution)/shard_map/all_to_all | solution.py:81
  166.3 0.3 reshape.134
  166.6 0.2 reduce_max.34
  166.8 0.3 reshape.136
  167.1 0.3 fusion.6
  167.4 38.4 %all-to-all-done.1 = bf16[1,2,2,4,128,512]{5,3,2,1,0,4:T(4,128)(2,1)S(1)} async-done(((bf16[1,2,2,4,128,512]{5,3,2,1,0,4:T(4,128)(2,1)}), bf16[1,2,2,4,128,512]{5,3,2,1,0,4:T(4,128)(2,1)S(1)}, u32[]{:S(2)}, u32[]{:S(2)}) %all-to-all-start.1) | async-done | bytes 2097184 | tf_op jit(solution)/shard_map/all_to_all | solution.py:97
  205.9 1.5 fusion
  207.4 0.3 divide_convert_fusion
  207.7 1.1 copy.71
  (23 shorter events, 0.2 us)
Async XLA Ops:
  7.2 113.9 %copy-start = (bf16[2,2,4,512]{3,2,1,0:T(4,128)(2,1)S(1)}, bf16[2,2,4,512]{3,2,1,0:T(4,128)(2,1)}, u32[]{:S(2)}) copy-start(bf16[2,2,4,512]{3,2,1,0:T(4,128)(2,1)} %param.14) | copy-start | bytes 49156
  7.2 113.9 %all-gather.2.cloned.1.call-start = ((), (), s32[]{:S(2)}) async-start(), calls=%async_computation.6 | async-start | bytes 2621440 | tf_op jit(solution)/shard_map/all_gather | solution.py:71
  10.6 11.9 %all-to-all-start.4 = ((bf16[2,2,128,4,4]{2,4,1,0,3:T(4,128)(2,1)}), bf16[2,2,128,4,4]{2,4,1,0,3:T(4,128)(2,1)S(1)}, u32[]{:S(2)}, u32[]{:S(2)}) async-start(bf16[2,2,128,4,4]{2,4,1,0,3:T(4,128)(2,1)} %copy.66), calls=%async_computation.4 | async-start | bytes 32768 | tf_op jit(solution)/shard_map/all_to_all | solution.py:82
  22.5 19.8 %all-to-all-start.5 = ((bf16[2,2,128,4,64]{2,4,1,0,3:T(8,128)(2,1)}), bf16[2,2,128,4,64]{2,4,1,0,3:T(8,128)(2,1)S(1)}, u32[]{:S(2)}, u32[]{:S(2)}) async-start(bf16[2,2,128,4,64]{2,4,1,0,3:T(8,128)(2,1)} %copy.69), calls=%async_computation.5 | async-start | bytes 524288 | tf_op jit(solution)/shard_map/all_to_all | solution.py:83
  30.8 5.6 %copy-start.2 = (bf16[2,2,512,512]{3,2,1,0:T(8,128)(2,1)S(1)}, bf16[2,2,512,512]{3,2,1,0:T(8,128)(2,1)}, u32[]{:S(2)}) copy-start(bf16[2,2,512,512]{3,2,1,0:T(8,128)(2,1)} %param.8) | copy-start | bytes 6291460
  38.6 8.2 %copy-start.4 = (bf16[2,2,4,32,64]{4,3,2,1,0:T(8,128)(2,1)S(1)}, bf16[2,2,4,32,64]{4,3,2,1,0:T(8,128)(2,1)}, u32[]{:S(2)}) copy-start(bf16[2,2,4,32,64]{4,3,2,1,0:T(8,128)(2,1)} %param.13) | copy-start | bytes 196612
  38.6 79.4 %copy-start.6 = (s32[2]{0:T(128)S(1)}, s32[2]{0:T(128)}, u32[]{:S(2)}) copy-start(s32[2]{0:T(128)} %param.11) | copy-start | bytes 28
  38.6 79.5 %copy-start.5 = (bf16[2,2,4,64]{3,2,1,0:T(4,128)(2,1)S(1)}, bf16[2,2,4,64]{3,2,1,0:T(4,128)(2,1)}, u32[]{:S(2)}) copy-start(bf16[2,2,4,64]{3,2,1,0:T(4,128)(2,1)} %param.15) | copy-start | bytes 6148
  38.6 79.7 %copy-start.3 = (bf16[2,2,512,64]{2,3,1,0:T(8,128)(2,1)S(1)}, bf16[2,2,512,64]{2,3,1,0:T(8,128)(2,1)}, u32[]{:S(2)}) copy-start(bf16[2,2,512,64]{2,3,1,0:T(8,128)(2,1)} %param.10) | copy-start | bytes 786436
  42.3 90.3 %all-to-all-start.3 = ((bf16[2,2,128,4,512]{4,2,1,0,3:T(8,128)(2,1)}), bf16[2,2,128,4,512]{4,2,1,0,3:T(8,128)(2,1)}, u32[]{:S(2)}, u32[]{:S(2)}) async-start(bf16[2,2,128,4,512]{4,2,1,0,3:T(8,128)(2,1)} %copy.64), calls=%async_computation.3 | async-start | bytes 4194304 | tf_op jit(solution)/shard_map/all_to_all | solution.py:81
  128.9 2.0 copy-start.1
  132.7 13.1 %all-to-all-start.2 = ((bf16[4,2,256]{2,1,0:T(2,128)(2,1)}), bf16[4,2,256]{2,1,0:T(2,128)(2,1)S(1)}, u32[]{:S(2)}, u32[]{:S(2)}) async-start(bf16[4,2,256]{2,1,0:T(2,128)(2,1)} %reshape.135), calls=%async_computation.2 | async-start | bytes 8192 | tf_op jit(solution)/shard_map/all_to_all | solution.py:99
  145.7 11.0 %all-to-all-start = ((bf16[4,2,256]{2,1,0:T(2,128)(2,1)}), bf16[4,2,256]{2,1,0:T(2,128)(2,1)S(1)}, u32[]{:S(2)}, u32[]{:S(2)}) async-start(bf16[4,2,256]{2,1,0:T(2,128)(2,1)} %reshape.133), calls=%async_computation | async-start | bytes 8192 | tf_op jit(solution)/shard_map/all_to_all | solution.py:98
  156.8 49.1 %all-to-all-start.1 = ((bf16[1,2,2,4,128,512]{5,3,2,1,0,4:T(4,128)(2,1)}), bf16[1,2,2,4,128,512]{5,3,2,1,0,4:T(4,128)(2,1)S(1)}, u32[]{:S(2)}, u32[]{:S(2)}) async-start(bf16[1,2,2,4,128,512]{5,3,2,1,0,4:T(4,128)(2,1)} %copy.61), calls=%async_computation.1 | async-start | bytes 4194304 | tf_op jit(solution)/shard_map/all_to_all | solution.py:97
Sparse Core Ops, SparseCore 0:
  9.6 73.4 all-gather.1
where the time goes:
time: 216 us
  blocking collectives  71.2 us (33%)
  waiting for transfers between devices  44.2 us (20%)
  local copies, waits for them, and re-layouts  32.4 us (15%)
  starting transfers between devices  29.4 us (14%)
  matrix products  20.9 us (10%)
  between operations  14.3 us (7%)
  other arithmetic  3.24 us (2%)
    all_gather x1, blocking collectives, per_device(): lax.all_gather(query_rope, 'seq', axis=3, tiled=True)  71.2 us
    all_to_all x1, waiting for transfers between devices, per_device(): lax.all_to_all(group_sum[None], 'seq', split_axis=4, concat_axis=0, tiled...  38.4 us
    mul x2, local copies, waits for them, and re-layouts, dequantize(): scaled = shaped * scale_values.astype(jnp.float32)[..., None]  9.47 us
    unnamed x22, local copies, waits for them, and re-layouts  9.29 us
    dot_general x1, matrix products, shard_partial(): group_sum = jnp.dot(weights, key_rows, preferred_element_type=jnp.float32)  7.14 us
    all_to_all x1, starting transfers between devices, per_device(): lax.all_to_all(regroup_rows(latent_scales), 'seq', split_axis=3, concat_a...  6.32 us
    reshape x4, local copies, waits for them, and re-layouts, regroup_rows(): values.reshape(values.shape[0], values.shape[1], span // shard_count, sha...  5.68 us
    dot_general x1, matrix products, shard_partial(): scores = jnp.dot(query_rows, key_rows.T, preferred_element_type=jnp.float32)  5.57 us
  transfers between devices with their start and end apart: 7, of which 3 were waited for; matrix products, arithmetic and copies ran while one was open for 24% of the time, Pallas kernels for 0%

commit v1 on v0

--- a/solution.py
+++ b/solution.py
@@ -95,7 +95,15 @@
     attended = merge_groups(
         (
             lax.all_to_all(group_sum[None], "seq", split_axis=4, concat_axis=0, tiled=True),
-            lax.all_to_all(group_peak[None], "seq", split_axis=4, concat_axis=0, tiled=True),
+            jnp.concatenate(
+                lax.all_to_all(
+                    jnp.stack(jnp.split(group_peak[None], lax.axis_size("seq"), axis=4), axis=0),
+                    "seq",
+                    0,
+                    0,
+                ),
+                axis=0,
+            ),
             lax.all_to_all(group_total[None], "seq", split_axis=4, concat_axis=0, tiled=True),
         )
     )

time: 216 us -> 201 us (0.931)
  blocking collectives: 71.2 us -> 31.6 us
  waiting for transfers between devices: 44.2 us -> 70.6 us
  starting transfers between devices: 29.4 us -> 26.4 us
  other arithmetic: 3.24 us -> 5.79 us
    all_gather x1, blocking collectives: 71.2 us -> 31.6 us  [per_device(): lax.all_gather(query_rope, 'seq', axis=3, tiled=True)]
    all_to_all x1, waiting for transfers between devices: 0.01 us -> 22.8 us  [per_device(): lax.all_to_all(regroup_rows(latent_codes), 'seq', split_axis=3, concat_ax...]
    all_to_all x1, waiting for transfers between devices: 0.01 us -> 4.58 us  [per_device(): lax.all_to_all(jnp.stack(jnp.split(group_peak[None], lax.axis_size('seq')...]
    reduce_sum x1, other arithmetic: 0.73 us -> 3.08 us  [shard_partial(): jnp.sum(weights.astype(jnp.float32), 1)]
    unnamed x22 -> x20, local copies, waits for them, and re-layouts: 9.29 us -> 7.4 us
  transfers between devices with their start and end apart: 7 -> 7, of which waited for: 3 -> 4; matrix products, arithmetic and copies ran while one was open for 24% -> 27% of each run, Pallas kernels for 0% -> 0%
where the time goes in v1:
time: 201 us
  waiting for transfers between devices  70.6 us (35%)
  blocking collectives  31.6 us (16%)
  local copies, waits for them, and re-layouts  30.3 us (15%)
  starting transfers between devices  26.4 us (13%)
  matrix products  21.6 us (11%)
  between operations  14.2 us (7%)
  other arithmetic  5.79 us (3%)
    all_to_all x1, waiting for transfers between devices, per_device(): lax.all_to_all(group_sum[None], 'seq', split_axis=4, concat_axis=0, tiled...  39.9 us
    all_gather x1, blocking collectives, per_device(): lax.all_gather(query_rope, 'seq', axis=3, tiled=True)  31.6 us
    all_to_all x1, waiting for transfers between devices, per_device(): lax.all_to_all(regroup_rows(latent_codes), 'seq', split_axis=3, concat_ax...  22.8 us
    mul x2, local copies, waits for them, and re-layouts, dequantize(): scaled = shaped * scale_values.astype(jnp.float32)[..., None]  9.46 us
    dot_general x1, matrix products, shard_partial(): scores = jnp.dot(query_rows, key_rows.T, preferred_element_type=jnp.float32)  7.53 us
    unnamed x20, local copies, waits for them, and re-layouts  7.4 us
    all_to_all x1, starting transfers between devices, per_device(): lax.all_to_all(regroup_rows(latent_scales), 'seq', split_axis=3, concat_a...  6.32 us
    dot_general x1, matrix products, shard_partial(): group_sum = jnp.dot(weights, key_rows, preferred_element_type=jnp.float32)  5.94 us
  transfers between devices with their start and end apart: 7, of which 4 were waited for; matrix products, arithmetic and copies ran while one was open for 27% of the time, Pallas kernels for 0%

profile of v1, /device:TPU:0, one launch (start us, length us, event | category | flops | bytes accessed | tf_op | source)
XLA Modules:
  0.0 200.6 jit_solution(10585755481284556585)
XLA Ops:
  7.2 0.0 all-gather.2.cloned.1.call-start
  7.2 0.7 all-gather.2.cloned.1.call-update
  7.9 1.8 reshape.127
  9.8 0.8 copy.119
  10.6 6.3 %all-to-all-start.4 = ((bf16[2,2,128,4,4]{2,4,1,0,3:T(4,128)(2,1)}), bf16[2,2,128,4,4]{2,4,1,0,3:T(4,128)(2,1)S(1)}, u32[]{:S(2)}, u32[]{:S(2)}) async-start(bf16[2,2,128,4,4]{2,4,1,0,3:T(4,128)(2,1)} %copy.119), calls=%async_computation.4 | async-start | bytes 32768 | tf_op jit(solution)/shard_map/all_to_all | solution.py:82
  16.9 0.7 broadcast_compare_fusion
  17.7 1.2 copy.121
  18.9 1.0 copy.122
  19.9 2.6 %all-to-all-done.4 = bf16[2,2,128,4,4]{2,4,1,0,3:T(4,128)(2,1)S(1)} async-done(((bf16[2,2,128,4,4]{2,4,1,0,3:T(4,128)(2,1)}), bf16[2,2,128,4,4]{2,4,1,0,3:T(4,128)(2,1)S(1)}, u32[]{:S(2)}, u32[]{:S(2)}) %all-to-all-start.4) | async-done | bytes 16416 | tf_op jit(solution)/shard_map/all_to_all | solution.py:82
  22.5 3.4 %all-to-all-start.5 = ((bf16[2,2,128,4,64]{2,4,1,0,3:T(8,128)(2,1)}), bf16[2,2,128,4,64]{2,4,1,0,3:T(8,128)(2,1)S(1)}, u32[]{:S(2)}, u32[]{:S(2)}) async-start(bf16[2,2,128,4,64]{2,4,1,0,3:T(8,128)(2,1)} %copy.122), calls=%async_computation.5 | async-start | bytes 524288 | tf_op jit(solution)/shard_map/all_to_all | solution.py:83
  26.0 31.6 %all_gather.7 = bf16[2,2,4,128,64]{4,3,2,1,0:T(8,128)(2,1)S(1)} all-gather(bf16[2,2,4,32,64]{4,3,2,1,0:T(8,128)(2,1)} %param.13), channel_id=1, replica_groups=mesh['group'=2,'seq'=4,'req'=2,'sub'=2] {'seq'}, dimensions={3}, use_global_device_ids=true | all-gather | bytes 327680 | tf_op jit(solution)/shard_map/all_gather | solution.py:72
  57.6 0.3 copy.107
  57.8 3.9 %mul.38 = f32[2,2,512,4,128]{4,3,2,1,0:T(4,128)} broadcast(f32[2,2,512,4]{3,2,1,0:T(8,128)S(1)} %copy.107), dimensions={0,1,2,3} | broadcast | bytes 4227072 | tf_op jit(solution)/shard_map/mul | solution.py:16
  61.7 5.6 %mul.39 = f32[2,2,512,512]{3,2,1,0:T(8,128)} reshape(f32[2,2,512,4,128]{4,3,2,1,0:T(4,128)} %mul.38) | data formatting | bytes 8388608 | tf_op jit(solution)/shard_map/mul | solution.py:16
  67.3 2.2 %copy.116 = bf16[2,2,512,512]{3,1,2,0:T(2,128)(2,1)S(1)} copy(bf16[2,2,512,512]{3,2,1,0:T(8,128)(2,1)S(1)} %copy-done.2) | data formatting | bytes 4194304 | tf_op args[0]
  69.5 2.0 copy.117
  71.5 0.2 fusion.17
  71.7 4.5 %all-to-all-start.3 = ((bf16[2,2,128,4,512]{4,2,1,0,3:T(8,128)(2,1)}), bf16[2,2,128,4,512]{4,2,1,0,3:T(8,128)(2,1)}, u32[]{:S(2)}, u32[]{:S(2)}) async-start(bf16[2,2,128,4,512]{4,2,1,0,3:T(8,128)(2,1)} %copy.117), calls=%async_computation.3 | async-start | bytes 4194304 | tf_op jit(solution)/shard_map/all_to_all | solution.py:81
  76.3 2.7 %fusion.16 = f32[2,2,512,512]{2,3,1,0:T(8,128)} fusion(bf16[2,2,512,64]{3,2,1,0:T(8,128)(2,1)S(1)} %bitcast.80, bf16[2,2,512,64]{2,3,1,0:T(8,128)(2,1)S(1)} %copy-done.3), kind=kOutput, calls=%fused_computation.44 | convolution fusion | flops 134217728 | bytes 4718592 | tf_op jit(solution)/shard_map/vmap(vmap())/dot_general | solution.py:28
  79.0 2.3 %fusion.15 = (bf16[2,2,512]{2,1,0:T(2,128)(2,1)S(1)}, f32[2,2,512,4]{2,3,1,0:T(4,128)S(1)}) fusion(f32[2,2,512,4]{2,3,1,0:T(4,128)S(1)} %fusion.17, bf16[2,2,512,512]{3,2,1,0:T(8,128)(2,1)} %bitcast.77, bf16[2,2,4,512]{3,2,1,0:T(4,128)(2,1)S(1)} %copy-done, pred[512,4]{0,1:T(4,128)(4,1)S(1)} %fusion.8), kind=kOutput, calls=%fused_computation.43 | convolution fusion | flops 8419328 | bytes 2185216 | tf_op jit(solution)/shard_map/vmap(vmap())/dot_general | solution.py:30
  81.3 7.5 %fusion.14 = (bf16[2,2,512]{2,1,0:T(2,128)(2,1)S(1)}, f32[2,2,512,512]{2,3,1,0:T(8,128)}) fusion(f32[2,2,512,512]{2,3,1,0:T(8,128)} %fusion.16, bf16[2,2,512,512]{3,2,1,0:T(8,128)(2,1)} %bitcast.78, f32[2,2,512,512]{3,2,1,0:T(8,128)} %mul.39, bf16[2,2,512,512]{3,2,1,0:T(8,128)(2,1)S(1)} %copy-done.2, pred[2,512]{1,0:T(4,128)(4,1)S(1)} %broadcast_compare_fusion), kind=kOutput, calls=%fused_computation.42 | convolution fusion | flops 1081079808 | bytes 16782336 | tf_op jit(solution)/shard_map/vmap(vmap())/dot_general | solution.py:26
  88.8 0.1 slice_bitcast_fusion.3
  88.9 0.7 reshape.136
  89.7 3.1 %convert_reduce_fusion = f32[2,2,512]{2,1,0:T(2,128)S(1)} fusion(f32[2,2,512,512]{2,3,1,0:T(8,128)} %get-tuple-element.37, f32[2,2,512]{2,1,0:T(2,128)S(1)} %get-tuple-element.28, pred[2,512]{1,0:T(4,128)(4,1)S(1)} %broadcast_compare_fusion), kind=kLoop, calls=%fused_computation.5 | loop fusion | flops 5240832 | bytes 4211712 | tf_op jit(solution)/shard_map/vmap(vmap())/reduce_sum | solution.py:42
  92.7 0.3 copy-done.1
  93.1 5.9 %fusion.5 = f32[2,2,512,512]{3,2,1,0:T(8,128)} fusion(f32[2,2,512,512]{2,3,1,0:T(8,128)} %get-tuple-element.37, f32[2,2,512]{2,1,0:T(2,128)S(1)} %get-tuple-element.28, pred[2,512]{1,0:T(4,128)(4,1)S(1)} %broadcast_compare_fusion, f32[2,2,512,512]{3,2,1,0:T(8,128)S(1)} %copy-done.1, bf16[2,2,512,512]{3,2,1,0:T(8,128)(2,1)S(1)} %copy-done.2), kind=kOutput, calls=%fused_computation.13 | convolution fusion | flops 1080033280 | bytes 14689280 | tf_op jit(solution)/shard_map/vmap(vmap())/dot_general | solution.py:45
  99.0 22.8 %all-to-all-done.3 = bf16[2,2,128,4,512]{4,2,1,0,3:T(8,128)(2,1)} async-done(((bf16[2,2,128,4,512]{4,2,1,0,3:T(8,128)(2,1)}), bf16[2,2,128,4,512]{4,2,1,0,3:T(8,128)(2,1)}, u32[]{:S(2)}, u32[]{:S(2)}) %all-to-all-start.3) | async-done | bytes 2097184 | tf_op jit(solution)/shard_map/all_to_all | solution.py:81
  121.8 3.8 %all-to-all-start = ((bf16[4,2,256]{2,1,0:T(2,128)(2,1)}), bf16[4,2,256]{2,1,0:T(2,128)(2,1)S(1)}, u32[]{:S(2)}, u32[]{:S(2)}) async-start(bf16[4,2,256]{2,1,0:T(2,128)(2,1)} %reshape.136), calls=%async_computation | async-start | bytes 8192 | tf_op jit(solution)/shard_map/all_to_all | solution.py:99
  125.7 0.2 copy.112
  125.8 0.8 reshape.134
  126.6 4.6 %all-to-all-done = bf16[4,2,256]{2,1,0:T(2,128)(2,1)S(1)} async-done(((bf16[4,2,256]{2,1,0:T(2,128)(2,1)}), bf16[4,2,256]{2,1,0:T(2,128)(2,1)S(1)}, u32[]{:S(2)}, u32[]{:S(2)}) %all-to-all-start) | async-done | bytes 4128 | tf_op jit(solution)/shard_map/all_to_all | solution.py:99
  131.2 3.4 %all-to-all-start.2 = ((bf16[4,2,256]{2,1,0:T(2,128)(2,1)}), bf16[4,2,256]{2,1,0:T(2,128)(2,1)S(1)}, u32[]{:S(2)}, u32[]{:S(2)}) async-start(bf16[4,2,256]{2,1,0:T(2,128)(2,1)} %reshape.134), calls=%async_computation.2 | async-start | bytes 8192 | tf_op jit(solution)/shard_map/all_to_all | solution.py:107
  134.6 3.0 %add_convert_fusion = bf16[2,2,512,512]{3,2,1,0:T(8,128)(2,1)S(1)} fusion(f32[2,2,512,512]{3,2,1,0:T(8,128)} %fusion.5, bf16[2,2,4,512]{3,2,1,0:T(4,128)(2,1)S(1)} %copy-done, f32[2,2,512,4]{2,3,1,0:T(4,128)S(1)} %get-tuple-element.39, f32[2,2,512]{2,1,0:T(2,128)S(1)} %get-tuple-element.28, pred[512,4]{0,1:T(4,128)(4,1)S(1)} %fusion.8), kind=kOutput, calls=%fused_computation.6 | convolution fusion | flops 10510336 | bytes 6350848 | tf_op jit(solution)/shard_map/vmap(vmap())/dot_general | solution.py:46
  137.6 3.0 %copy.111 = bf16[1,2,2,4,128,512]{5,3,2,1,0,4:T(4,128)(2,1)} copy(bf16[1,2,2,4,128,512]{5,4,3,2,1,0:T(8,128)(2,1)S(1)} %bitcast.75) | data formatting | bytes 4194304 | tf_op jit(solution)/shard_map/broadcast_in_dim;vmap(vmap())/reshape | solution.py:97
  140.6 4.9 %all-to-all-start.1 = ((bf16[1,2,2,4,128,512]{5,3,2,1,0,4:T(4,128)(2,1)}), bf16[1,2,2,4,128,512]{5,3,2,1,0,4:T(4,128)(2,1)S(1)}, u32[]{:S(2)}, u32[]{:S(2)}) async-start(bf16[1,2,2,4,128,512]{5,3,2,1,0,4:T(4,128)(2,1)} %copy.111), calls=%async_computation.1 | async-start | bytes 4194304 | tf_op jit(solution)/shard_map/all_to_all | solution.py:97
  145.4 0.6 copy_bitcast_fusion
  146.1 0.7 bitcast_bitcast_fusion
  146.8 3.1 %copy.118 = bf16[2,2,128,4,512]{4,2,3,1,0:T(8,128)(2,1)} copy(bf16[2,2,128,4,512]{4,2,1,0,3:T(8,128)(2,1)} %all-to-all-done.3) | data formatting | bytes 4194304 | tf_op jit(solution)/shard_map/all_to_all | solution.py:81
  149.9 0.1 reshape.137
  150.0 0.3 reshape.135
  150.3 0.1 copy.113
  150.4 0.1 reshape.133
  150.5 0.2 copy.109
  150.8 0.1 copy.115
  150.9 39.9 %all-to-all-done.1 = bf16[1,2,2,4,128,512]{5,3,2,1,0,4:T(4,128)(2,1)S(1)} async-done(((bf16[1,2,2,4,128,512]{5,3,2,1,0,4:T(4,128)(2,1)}), bf16[1,2,2,4,128,512]{5,3,2,1,0,4:T(4,128)(2,1)S(1)}, u32[]{:S(2)}, u32[]{:S(2)}) %all-to-all-start.1) | async-done | bytes 2097184 | tf_op jit(solution)/shard_map/all_to_all | solution.py:97
  190.8 1.5 fusion
  192.4 0.3 divide_convert_fusion
  192.6 1.1 copy.124
  (26 shorter events, 0.2 us)
Async XLA Ops:
  7.2 71.8 %copy-start = (bf16[2,2,4,512]{3,2,1,0:T(4,128)(2,1)S(1)}, bf16[2,2,4,512]{3,2,1,0:T(4,128)(2,1)}, u32[]{:S(2)}) copy-start(bf16[2,2,4,512]{3,2,1,0:T(4,128)(2,1)} %param.14) | copy-start | bytes 49156
  7.2 50.4 %copy-start.4 = (bf16[2,2,512,4]{2,3,1,0:T(4,128)(2,1)S(1)}, bf16[2,2,512,4]{2,3,1,0:T(4,128)(2,1)}, u32[]{:S(2)}) copy-start(bf16[2,2,512,4]{2,3,1,0:T(4,128)(2,1)} %param.9) | copy-start | bytes 49156
  7.2 71.8 %all-gather.2.cloned.1.call-start = ((), (), s32[]{:S(2)}) async-start(), calls=%async_computation.6 | async-start | bytes 2621440 | tf_op jit(solution)/shard_map/all_gather | solution.py:71
  10.6 11.9 %all-to-all-start.4 = ((bf16[2,2,128,4,4]{2,4,1,0,3:T(4,128)(2,1)}), bf16[2,2,128,4,4]{2,4,1,0,3:T(4,128)(2,1)S(1)}, u32[]{:S(2)}, u32[]{:S(2)}) async-start(bf16[2,2,128,4,4]{2,4,1,0,3:T(4,128)(2,1)} %copy.119), calls=%async_computation.4 | async-start | bytes 32768 | tf_op jit(solution)/shard_map/all_to_all | solution.py:82
  22.5 49.2 %all-to-all-start.5 = ((bf16[2,2,128,4,64]{2,4,1,0,3:T(8,128)(2,1)}), bf16[2,2,128,4,64]{2,4,1,0,3:T(8,128)(2,1)S(1)}, u32[]{:S(2)}, u32[]{:S(2)}) async-start(bf16[2,2,128,4,64]{2,4,1,0,3:T(8,128)(2,1)} %copy.122), calls=%async_computation.5 | async-start | bytes 524288 | tf_op jit(solution)/shard_map/all_to_all | solution.py:83
  61.7 5.6 %copy-start.2 = (bf16[2,2,512,512]{3,2,1,0:T(8,128)(2,1)S(1)}, bf16[2,2,512,512]{3,2,1,0:T(8,128)(2,1)}, u32[]{:S(2)}) copy-start(bf16[2,2,512,512]{3,2,1,0:T(8,128)(2,1)} %param.8) | copy-start | bytes 6291460
  67.3 4.2 %copy-start.5 = (bf16[2,2,4,64]{3,2,1,0:T(4,128)(2,1)S(1)}, bf16[2,2,4,64]{3,2,1,0:T(4,128)(2,1)}, u32[]{:S(2)}) copy-start(bf16[2,2,4,64]{3,2,1,0:T(4,128)(2,1)} %param.15) | copy-start | bytes 6148
  69.5 6.8 %copy-start.3 = (bf16[2,2,512,64]{2,3,1,0:T(8,128)(2,1)S(1)}, bf16[2,2,512,64]{2,3,1,0:T(8,128)(2,1)}, u32[]{:S(2)}) copy-start(bf16[2,2,512,64]{2,3,1,0:T(8,128)(2,1)} %param.10) | copy-start | bytes 786436
  71.7 50.1 %all-to-all-start.3 = ((bf16[2,2,128,4,512]{4,2,1,0,3:T(8,128)(2,1)}), bf16[2,2,128,4,512]{4,2,1,0,3:T(8,128)(2,1)}, u32[]{:S(2)}, u32[]{:S(2)}) async-start(bf16[2,2,128,4,512]{4,2,1,0,3:T(8,128)(2,1)} %copy.117), calls=%async_computation.3 | async-start | bytes 4194304 | tf_op jit(solution)/shard_map/all_to_all | solution.py:81
  89.6 3.4 %copy-start.1 = (f32[2,2,512,512]{3,2,1,0:T(8,128)S(1)}, f32[2,2,512,512]{3,2,1,0:T(8,128)}, u32[]{:S(2)}) copy-start(f32[2,2,512,512]{3,2,1,0:T(8,128)} %mul.39) | copy-start | bytes 12582916
  121.8 9.4 %all-to-all-start = ((bf16[4,2,256]{2,1,0:T(2,128)(2,1)}), bf16[4,2,256]{2,1,0:T(2,128)(2,1)S(1)}, u32[]{:S(2)}, u32[]{:S(2)}) async-start(bf16[4,2,256]{2,1,0:T(2,128)(2,1)} %reshape.136), calls=%async_computation | async-start | bytes 8192 | tf_op jit(solution)/shard_map/all_to_all | solution.py:99
  131.2 9.4 %all-to-all-start.2 = ((bf16[4,2,256]{2,1,0:T(2,128)(2,1)}), bf16[4,2,256]{2,1,0:T(2,128)(2,1)S(1)}, u32[]{:S(2)}, u32[]{:S(2)}) async-start(bf16[4,2,256]{2,1,0:T(2,128)(2,1)} %reshape.134), calls=%async_computation.2 | async-start | bytes 8192 | tf_op jit(solution)/shard_map/all_to_all | solution.py:107
  140.6 50.2 %all-to-all-start.1 = ((bf16[1,2,2,4,128,512]{5,3,2,1,0,4:T(4,128)(2,1)}), bf16[1,2,2,4,128,512]{5,3,2,1,0,4:T(4,128)(2,1)S(1)}, u32[]{:S(2)}, u32[]{:S(2)}) async-start(bf16[1,2,2,4,128,512]{5,3,2,1,0,4:T(4,128)(2,1)} %copy.111), calls=%async_computation.1 | async-start | bytes 4194304 | tf_op jit(solution)/shard_map/all_to_all | solution.py:97
Sparse Core Ops, SparseCore 0:
  9.6 62.4 all-gather.1
